TPU v7x, 256 devices: a whole 4x4x8 slice. The times are simulated.
256 devices in a mesh: blk: 64 (over y, x, z_hi, core), grp: 4 (over z_lo).
Axes of the slice: x: 4, y: 4, z: 8 (z_hi: 2, z_lo: 4; z = z_hi * 4 + z_lo), core: 2. Of those that a mesh axis runs over, the one named last changes fastest.
Arguments:
- amplitudes: float32 [2048, 4, 65536], P('grp', None, 'blk'), may hold values from -6 to 6
- integrals: float32 [4, 65536, 256], P('grp', 'blk'), may hold values from -0.0234375 to 0.0234375
- irrep_sizes: int32 [4], replicated, may hold values from 86 to 256, as said below
- owner_map: int32 [4], replicated, may hold values from 0 to 3, each once
Outputs:
- ladder: float32 [2048, 4, 256], P('grp', None, 'blk')
Inputs may be any that keep to these rules, and one draw needn't show every extreme that they name: `irrep_sizes`: one irrep fills its block and one has the smallest size.
All inputs are finite; a program needn't handle non-finite values.
Results may differ from a plain program's by a relative error of at most 0.0001.
Values sent between devices are 32-bit elements; how exact they have to be, the bound alone decides.
No kernel may reach another device: no remote copies, remote signals or barrier semaphores. Data moves between devices by JAX's collectives and lax.ppermute only.
A program may use at most 128 MiB of HBM per device.

v0:
```python
import jax
import jax.numpy as jnp
from jax import lax
from jax.sharding import PartitionSpec as P

BLOCK = 256
IRREPS = 4


def from_root(shard, axis, root):
    mine = lax.axis_index(axis) == root
    return lax.psum(jnp.where(mine, shard, jnp.zeros_like(shard)), axis)


def slot_valid(irrep_sizes, offset, width):
    slot = offset + jnp.arange(width, dtype=jnp.int32)
    sizes = irrep_sizes[:, None]
    return ((slot[None, :] // BLOCK < sizes) & (slot[None, :] % BLOCK < sizes)).astype(jnp.float32)


def local(amplitudes, integrals, irrep_sizes, owner_map):
    slot_width = amplitudes.shape[2]
    column_width = integrals.shape[2] // lax.axis_size("blk")
    position = lax.axis_index("blk")
    row_valid = slot_valid(irrep_sizes, position * slot_width, slot_width)
    column_valid = slot_valid(irrep_sizes, position * column_width, column_width)
    masked = amplitudes * row_valid[None, :, :]
    blocks = []
    for irrep in range(IRREPS):
        slab_rows = from_root(integrals, "grp", owner_map[irrep])[0]
        blocks.append(
            jnp.dot(
                masked[:, irrep, :],
                slab_rows,
                precision=lax.Precision.HIGHEST,
                preferred_element_type=jnp.float32,
            )
        )
    partial_value = jnp.stack(blocks, axis=1)
    result = lax.psum_scatter(partial_value, "blk", scatter_dimension=2, tiled=True)
    return result * column_valid[None, :, :]


def solution(mesh):
    in_specs = (P("grp", None, "blk"), P("grp", "blk", None), P(), P())
    out_specs = P("grp", None, "blk")
    return jax.shard_map(local, mesh=mesh, in_specs=in_specs, out_specs=out_specs, check_vma=False)
```

profile of v0, /device:TPU:1, one launch (start us, length us, event | category | flops | bytes accessed | tf_op | source)
XLA Modules:
  0.0 1000.0 jit_solution(15541328283892642709)
XLA Ops:
  6.5 0.0 all-reduce.7.cloned.1.call-start
  6.5 1.4 fusion.13
  10.5 3.3 select_bitcast_fusion.3
  13.7 0.0 copy-start.3
  13.7 0.0 all-reduce.7.cloned.1.call-update
  13.7 0.0 all-reduce.5.cloned.1.call-start
  13.8 0.6 copy-done.3
  14.4 0.1 and_convert_fusion
  14.4 11.5 %copy_multiply_fusion = f32[512,4,1024]{2,0,1:T(8,128)} fusion(f32[512,4,1024]{2,1,0:T(4,128)} %param.4, f32[4,1024]{1,0:T(4,128)S(1)} %and_convert_fusion), kind=kLoop, calls=%fused_computation | loop fusion | flops 2097152 | bytes 16793600 | tf_op jit(solution)/shard_map/mul | solution.py:27
  25.9 156.1 %all-reduce.7.cloned.1.call-done = (f32[1024,256]{1,0:T(8,128)}, f32[1024,256]{1,0:T(8,128)}, f32[1024,256]{1,0:T(8,128)}, f32[1024,256]{1,0:T(8,128)}) async-done(((f32[1024,256]{1,0:T(8,128)}, f32[1024,256]{1,0:T(8,128)}, f32[1024,256]{1,0:T(8,128)}, f32[1024,256]{1,0:T(8,128)}), (f32[1024,256]{1,0:T(8,128)}, f32[1024,256]{1,0:T(8,128)}, f32[1024,256]{1,0:T(8,128)}, ...) | async-done | bytes 4194320 | tf_op jit(solution)/shard_map/psum | solution.py:12
  182.0 0.0 copy-start.2
  182.0 3.7 fusion.4
  185.7 0.0 copy-start.1
  185.7 0.0 copy-done.2
  185.8 3.5 fusion.5
  189.2 0.0 copy-start
  189.3 0.0 copy-done.1
  189.3 3.5 fusion.6
  192.8 0.0 copy-done
  192.8 3.4 fusion.7
  196.2 0.1 pad_maximum_fusion
  196.3 2.0 copy.9
  198.3 0.0 copy-start.4
  198.3 0.0 all-reduce.5.cloned.1.call-update
  198.4 0.6 copy-done.4
  199.0 0.6 dynamic-slice
  200.3 0.1 and_convert_fusion.1
  200.3 791.4 %all-reduce.5.cloned.1.call-done = f32[512,4,256]{0,1,2:T(4,128)} async-done(((f32[512,4,256]{0,1,2:T(4,128)}), f32[512,4,256]{0,1,2:T(4,128)}) %all-reduce.5.cloned.1.call-update) | async-done | bytes 2097168
  991.7 0.8 dynamic-slice_multiply_fusion
  992.6 0.6 copy.10
  (2 shorter events, 0.0 us)
Async XLA Ops:
  6.5 175.5 %all-reduce.7.cloned.1.call-start = ((), (), s32[]{:S(2)}) async-start(), calls=%async_computation.1 | async-start | bytes 8388608 | tf_op jit(solution)/shard_map/psum | solution.py:12
  13.7 0.7 copy-start.3
  13.7 978.0 %all-reduce.5.cloned.1.call-start = ((), (), s32[]{:S(2)}) async-start(), calls=%async_computation | async-start | bytes 4194304
  182.0 3.8 copy-start.2
  185.7 3.5 copy-start.1
  189.2 3.5 copy-start
  198.3 0.7 copy-start.4
Sparse Core Ops, SparseCore 0:
  13.9 168.0 all-reduce.6
  198.5 793.2 all-reduce.4
where the time goes:
time: 1000 us
  waiting for transfers between devices  948 us (95%)
  between operations  16.6 us (2%)
  other arithmetic  15.9 us (2%)
  matrix products  14.1 us (1%)
    unnamed x3, waiting for transfers between devices  791 us
    psum x1, waiting for transfers between devices, from_root(): return lax.psum(jnp.where(mine, shard, jnp.zeros_like(shard)), axis)  156 us
  transfers between devices with their start and end apart: 2, of which 2 were waited for; matrix products, arithmetic and copies ran while one was open for 1% of the time, Pallas kernels for 0%

commit v1 on v0

--- a/solution.py
+++ b/solution.py
@@ -9,7 +9,7 @@
 
 def from_root(shard, axis, root):
     mine = lax.axis_index(axis) == root
-    return lax.psum(jnp.where(mine, shard, jnp.zeros_like(shard)), axis)
+    return jnp.sum(lax.all_gather(jnp.where(mine, shard, jnp.zeros_like(shard)), axis), axis=0)
 
 
 def slot_valid(irrep_sizes, offset, width):

time: 1000 us -> 1170 us (1.17)
  waiting for transfers between devices: 948 us -> 1110 us
    all_gather x0 -> x4, waiting for transfers between devices: none -> 312 us  [from_root(): lax.all_gather(jnp.where(mine, shard, jnp.zeros_like(shard)), axis)]
    psum x1 -> x0, waiting for transfers between devices: 156 us -> none  [from_root(): return lax.psum(jnp.where(mine, shard, jnp.zeros_like(shard)), axis)]
    unnamed x3 -> x6, waiting for transfers between devices: 791 us -> 793 us
  transfers between devices with their start and end apart: 2 -> 5, of which waited for: 2 -> 5; matrix products, arithmetic and copies ran while one was open for 1% -> 3% of each run, Pallas kernels for 0% -> 0%
where the time goes in v1:
time: 1170 us
  waiting for transfers between devices  1110 us (95%)
  other arithmetic  26.3 us (2%)
  between operations  16.5 us (1%)
  matrix products  15.5 us (1%)
    unnamed x6, waiting for transfers between devices  793 us
    all_gather x4, waiting for transfers between devices, from_root(): lax.all_gather(jnp.where(mine, shard, jnp.zeros_like(shard)), axis)  312 us
  transfers between devices with their start and end apart: 5, of which 5 were waited for; matrix products, arithmetic and copies ran while one was open for 3% of the time, Pallas kernels for 0%

profile of v1, /device:TPU:1, one launch (start us, length us, event | category | flops | bytes accessed | tf_op | source)
XLA Modules:
  0.0 1169.0 jit_solution(7144266580854369798)
XLA Ops:
  6.5 0.0 all-gather.11.cloned.1.call-start
  6.5 1.5 fusion.13
  10.6 3.3 broadcast_select_fusion.3
  13.9 0.0 copy-start.2
  13.9 0.0 all-gather.11.cloned.1.call-update
  14.0 0.0 all-gather.15.cloned.1.call-start
  14.0 0.7 all-gather.15.cloned.1.call-update
  14.7 0.0 all-gather.13.cloned.1.call-start
  14.8 0.7 all-gather.13.cloned.1.call-update
  15.4 0.0 all-gather.9.cloned.1.call-start
  15.5 0.5 all-gather.9.cloned.1.call-update
  16.0 0.0 all-reduce.3.cloned.1.call-start
  16.1 0.0 copy-done.2
  16.1 0.1 and_convert_fusion
  16.2 11.5 copy_multiply_fusion
  27.6 74.0 %all-gather.11.cloned.1.call-done = f32[4,1024,256]{2,1,0:T(8,128)} async-done(((f32[1,1024,256]{2,1,0:T(8,128)}), f32[4,1024,256]{2,1,0:T(8,128)}) %all-gather.11.cloned.1.call-update) | async-done | bytes 4194320 | tf_op jit(solution)/shard_map/all_gather | solution.py:12
  101.6 2.6 reduce.5
  104.2 83.3 %all-gather.15.cloned.1.call-done = f32[4,1024,256]{2,1,0:T(8,128)} async-done(((f32[1,1024,256]{2,1,0:T(8,128)}), f32[4,1024,256]{2,1,0:T(8,128)}) %all-gather.15.cloned.1.call-update) | async-done | bytes 4194320 | tf_op jit(solution)/shard_map/all_gather | solution.py:12
  187.5 2.6 reduce.7
  190.1 83.3 %all-gather.13.cloned.1.call-done = f32[4,1024,256]{2,1,0:T(8,128)} async-done(((f32[1,1024,256]{2,1,0:T(8,128)}), f32[4,1024,256]{2,1,0:T(8,128)}) %all-gather.13.cloned.1.call-update) | async-done | bytes 4194320 | tf_op jit(solution)/shard_map/all_gather | solution.py:12
  273.5 2.6 reduce.6
  276.0 4.2 fusion.7
  280.3 4.2 fusion.6
  284.5 3.6 fusion.5
  288.1 71.1 %all-gather.9.cloned.1.call-done = f32[4,1024,256]{2,1,0:T(8,128)} async-done(((f32[1,1024,256]{2,1,0:T(8,128)}), f32[4,1024,256]{2,1,0:T(8,128)}) %all-gather.9.cloned.1.call-update) | async-done | bytes 4194320 | tf_op jit(solution)/shard_map/all_gather | solution.py:12
  359.2 2.6 reduce.4
  361.8 0.0 copy-start
  361.8 0.0 copy-start.1
  361.8 3.5 fusion.4
  365.3 0.0 copy-done
  365.3 0.0 copy-done.1
  365.3 0.1 pad_maximum_fusion
  365.5 2.0 copy.9
  367.5 0.0 copy-start.3
  367.5 0.0 all-reduce.3.cloned.1.call-update
  367.5 0.6 copy-done.3
  368.1 0.6 dynamic-slice
  369.4 0.1 and_convert_fusion.1
  369.5 791.6 %all-reduce.3.cloned.1.call-done = f32[512,4,256]{0,1,2:T(4,128)} async-done(((f32[512,4,256]{0,1,2:T(4,128)}), f32[512,4,256]{0,1,2:T(4,128)}) %all-reduce.3.cloned.1.call-update) | async-done | bytes 2097168
  1161.0 0.8 dynamic-slice_multiply_fusion
  1161.9 0.6 copy.10
  (2 shorter events, 0.0 us)
Async XLA Ops:
  6.5 95.1 %all-gather.11.cloned.1.call-start = ((), (), s32[]{:S(2)}) async-start(), calls=%async_computation.1 | async-start | bytes 5242880 | tf_op jit(solution)/shard_map/all_gather | solution.py:12
  13.9 2.2 copy-start.2
  14.0 173.6 %all-gather.15.cloned.1.call-start = ((), (), s32[]{:S(2)}) async-start(), calls=%async_computation.3 | async-start | bytes 5242880 | tf_op jit(solution)/shard_map/all_gather | solution.py:12
  14.7 258.7 %all-gather.13.cloned.1.call-start = ((), (), s32[]{:S(2)}) async-start(), calls=%async_computation.2 | async-start | bytes 5242880 | tf_op jit(solution)/shard_map/all_gather | solution.py:12
  15.4 343.8 %all-gather.9.cloned.1.call-start = ((), (), s32[]{:S(2)}) async-start(), calls=%async_computation | async-start | bytes 5242880 | tf_op jit(solution)/shard_map/all_gather | solution.py:12
  16.0 1145.0 %all-reduce.3.cloned.1.call-start = ((), (), s32[]{:S(2)}) async-start(), calls=%async_computation.4 | async-start | bytes 4194304
  361.8 3.5 copy-start
  361.8 3.5 copy-start.1
  367.5 0.7 copy-start.3
Sparse Core Ops, SparseCore 0:
  14.1 87.5 all-gather.10
  103.4 84.0 all-gather.14
  189.4 84.0 all-gather.12
  275.1 84.0 all-gather.8
  367.6 793.3 all-reduce.2
